TPU v7x, 32 devices: a whole 2x2x4 slice. The times are simulated.
32 devices in a mesh: replica: 8 (over z, y), shard: 4 (over x, core).
Axes of the slice: x: 2, y: 2, z: 4, core: 2. Of those that a mesh axis runs over, the one named last changes fastest.
Arguments:
- hidden_in: bfloat16 [4096, 1024], P(('replica', 'shard')), may hold values from -6 to 6
- out_grad: bfloat16 [4096, 1024], P(('replica', 'shard')), may hold values from -6 to 6
- lengths: int32 [32, 4], P(('replica', 'shard')), may hold values from 1 to 64, 128 in all within a row
- norm1_gain: bfloat16 [1024], P('shard'), may hold values from 0.099609375 to 1.8984375
- norm1_bias: bfloat16 [1024], P('shard'), may hold values from -3 to 3
- qkv_weight: bfloat16 [1024, 3072], P('shard'), may hold values from -0.1875 to 0.1875
- query_bias: bfloat16 [1024], P('shard'), may hold values from -3 to 3
- value_bias: bfloat16 [1024], P('shard'), may hold values from -3 to 3
- out_weight: bfloat16 [1024, 1024], P('shard'), may hold values from -0.75 to 0.75
- out_bias: bfloat16 [1024], P('shard'), may hold values from -3 to 3
- norm2_gain: bfloat16 [1024], P('shard'), may hold values from 0.099609375 to 1.8984375
- norm2_bias: bfloat16 [1024], P('shard'), may hold values from -3 to 3
- up_weight: bfloat16 [1024, 4096], P('shard'), may hold values from -0.1875 to 0.1875
- up_bias: bfloat16 [4096], P('shard'), may hold values from -3 to 3
- down_weight: bfloat16 [4096, 1024], P('shard'), may hold values from -0.125 to 0.125
- down_bias: bfloat16 [1024], P('shard'), may hold values from -3 to 3
Outputs:
- hidden_out: bfloat16 [4096, 1024], P(('replica', 'shard'))
- in_grad: bfloat16 [4096, 1024], P(('replica', 'shard'))
- norm1_gain_grad: float32 [1024], P('shard')
- norm1_bias_grad: float32 [1024], P('shard')
- qkv_weight_grad: float32 [1024, 3072], P('shard')
- query_bias_grad: float32 [1024], P('shard')
- value_bias_grad: float32 [1024], P('shard')
- out_weight_grad: float32 [1024, 1024], P('shard')
- out_bias_grad: float32 [1024], P('shard')
- norm2_gain_grad: float32 [1024], P('shard')
- norm2_bias_grad: float32 [1024], P('shard')
- up_weight_grad: float32 [1024, 4096], P('shard')
- up_bias_grad: float32 [4096], P('shard')
- down_weight_grad: float32 [4096, 1024], P('shard')
- down_bias_grad: float32 [1024], P('shard')
Inputs may be any that keep to these rules, and one draw needn't show every extreme that they name: The 4 lengths of each device add up to 128, and the largest of all is 64.
All inputs are finite; a program needn't handle non-finite values.
Results may differ from a plain program's by a relative error of at most 0.018.
Values may be sent and summed in bfloat16 or wider, within the bound.
A program may use at most 192 MiB of HBM per device.

v0:
```python
import math
import jax
import jax.numpy as jnp
from jax import lax
from jax.sharding import PartitionSpec as P

HEADS = 16
HEAD_DIM = 64
EPSILON = 1e-05
TANH_SCALE = math.sqrt(2.0 / math.pi)
CUBIC = 0.044715


def product(left, right):
    return jnp.dot(left, right, preferred_element_type=jnp.float32)


def left_product(left, right):
    return lax.dot_general(
        left, right, (((0,), (0,)), ((), ())), preferred_element_type=jnp.float32
    )


def right_product(left, right):
    return lax.dot_general(
        left, right, (((1,), (1,)), ((), ())), preferred_element_type=jnp.float32
    )


def column_term(left, right):
    return left_product(left, right)


def gelu_parts(pre_act):
    inner_arg = TANH_SCALE * (pre_act + CUBIC * pre_act * pre_act * pre_act)
    tangent = jnp.tanh(inner_arg)
    gelu_value = 0.5 * pre_act * (1.0 + tangent)
    gelu_slope = 0.5 * (1.0 + tangent) + 0.5 * pre_act * (1.0 - tangent * tangent) * TANH_SCALE * (
        1.0 + 3.0 * CUBIC * pre_act * pre_act
    )
    return (gelu_value, gelu_slope)


def layer_norm(inputs, gain_row, bias_row):
    average = jnp.mean(inputs, axis=-1, keepdims=True)
    centred = inputs - average
    inv_std = lax.rsqrt(jnp.mean(centred * centred, axis=-1, keepdims=True) + EPSILON)
    normed = centred * inv_std
    return (normed * gain_row.astype(jnp.float32) + bias_row.astype(jnp.float32), normed, inv_std)


def norm_back(upstream, normed, inv_std, gain_row):
    scaled = upstream * gain_row.astype(jnp.float32)
    first_term = jnp.mean(scaled, axis=-1, keepdims=True)
    second_term = jnp.mean(scaled * normed, axis=-1, keepdims=True)
    input_grad = inv_std * (scaled - first_term - normed * second_term)
    return (input_grad, jnp.sum(upstream * normed, axis=0), jnp.sum(upstream, axis=0))


def seq_mask(lengths, row_count):
    seq_ends = jnp.cumsum(lengths, axis=-1)
    places = jnp.arange(row_count, dtype=jnp.int32)
    segment = jnp.sum((places[None, :, None] >= seq_ends[:, None, :]).astype(jnp.int32), axis=-1)
    causal = places[None, :] <= places[:, None]
    return (segment[:, :, None] == segment[:, None, :]) & causal[None]


def split_heads(flat_rows, groups):
    return flat_rows.reshape(groups, -1, HEADS, HEAD_DIM)


def attend_forward(queries, key_rows, values, allowed):
    groups = allowed.shape[0]
    scale_factor = 1.0 / math.sqrt(HEAD_DIM)
    head_q = split_heads(queries, groups)
    head_k = split_heads(key_rows, groups)
    head_v = split_heads(values, groups)
    scores = (
        jnp.einsum("gqhd,gkhd->ghqk", head_q, head_k, preferred_element_type=jnp.float32)
        * scale_factor
    )
    visible = allowed[:, None]
    row_total = jnp.sum(jnp.where(visible, jnp.exp(scores), 0.0), axis=-1, keepdims=True)
    log_total = jnp.log(row_total)
    probs_round = jnp.where(visible, jnp.exp(scores - log_total), 0.0).astype(jnp.bfloat16)
    context = jnp.einsum("ghqk,gkhd->gqhd", probs_round, head_v, preferred_element_type=jnp.float32)
    return (context.reshape(-1, HEADS * HEAD_DIM).astype(jnp.bfloat16), log_total)


def attend_backward(queries, key_rows, values, allowed, log_total, context_grad):
    groups = allowed.shape[0]
    scale_factor = 1.0 / math.sqrt(HEAD_DIM)
    head_q = split_heads(queries, groups)
    head_k = split_heads(key_rows, groups)
    head_v = split_heads(values, groups)
    head_g = split_heads(context_grad, groups)
    scores = (
        jnp.einsum("gqhd,gkhd->ghqk", head_q, head_k, preferred_element_type=jnp.float32)
        * scale_factor
    )
    visible = allowed[:, None]
    exact_probs = jnp.where(visible, jnp.exp(scores - log_total), 0.0)
    probs_round = exact_probs.astype(jnp.bfloat16)
    prob_grad = jnp.einsum("gqhd,gkhd->ghqk", head_g, head_v, preferred_element_type=jnp.float32)
    value_grad = jnp.einsum(
        "ghqk,gqhd->gkhd", probs_round, head_g, preferred_element_type=jnp.float32
    )
    row_delta = jnp.sum(exact_probs * prob_grad, axis=-1, keepdims=True)
    score_grad = (exact_probs * (prob_grad - row_delta) * scale_factor).astype(jnp.bfloat16)
    query_grad = jnp.einsum(
        "ghqk,gkhd->gqhd", score_grad, head_k, preferred_element_type=jnp.float32
    )
    key_grad = jnp.einsum("ghqk,gqhd->gkhd", score_grad, head_q, preferred_element_type=jnp.float32)
    model_width = HEADS * HEAD_DIM
    return (
        query_grad.reshape(-1, model_width),
        key_grad.reshape(-1, model_width),
        value_grad.reshape(-1, model_width),
    )


def local(
    hidden_in,
    out_grad,
    lengths,
    norm1_gain,
    norm1_bias,
    qkv_weight,
    query_bias,
    value_bias,
    out_weight,
    out_bias,
    norm2_gain,
    norm2_bias,
    up_weight,
    up_bias,
    down_weight,
    down_bias,
):
    (
        gain_one,
        bias_one,
        qkv_full,
        qbias_full,
        vbias_full,
        outw_full,
        outb_full,
        gain_two,
        bias_two,
        upw_full,
        upb_full,
        downw_full,
        downb_full,
    ) = (
        lax.all_gather(norm1_gain, "shard", axis=0, tiled=True),
        lax.all_gather(norm1_bias, "shard", axis=0, tiled=True),
        lax.all_gather(qkv_weight, "shard", axis=0, tiled=True),
        lax.all_gather(query_bias, "shard", axis=0, tiled=True),
        lax.all_gather(value_bias, "shard", axis=0, tiled=True),
        lax.all_gather(out_weight, "shard", axis=0, tiled=True),
        lax.all_gather(out_bias, "shard", axis=0, tiled=True),
        lax.all_gather(norm2_gain, "shard", axis=0, tiled=True),
        lax.all_gather(norm2_bias, "shard", axis=0, tiled=True),
        lax.all_gather(up_weight, "shard", axis=0, tiled=True),
        lax.all_gather(up_bias, "shard", axis=0, tiled=True),
        lax.all_gather(down_weight, "shard", axis=0, tiled=True),
        lax.all_gather(down_bias, "shard", axis=0, tiled=True),
    )
    allowed = seq_mask(lengths, hidden_in.shape[0])
    model_width = hidden_in.shape[1]
    inputs_wide = hidden_in.astype(jnp.float32)
    first_out, normed_one, inv_one = layer_norm(inputs_wide, gain_one, bias_one)
    first_in = first_out.astype(jnp.bfloat16)
    projected = product(first_in, qkv_full)
    queries = (projected[:, :model_width] + qbias_full.astype(jnp.float32)).astype(jnp.bfloat16)
    key_rows = projected[:, model_width : 2 * model_width].astype(jnp.bfloat16)
    values = (projected[:, 2 * model_width :] + vbias_full.astype(jnp.float32)).astype(jnp.bfloat16)
    context, log_total = attend_forward(queries, key_rows, values, allowed)
    residual = inputs_wide + product(context, outw_full) + outb_full.astype(jnp.float32)
    second_out, normed_two, inv_two = layer_norm(residual, gain_two, bias_two)
    second_in = second_out.astype(jnp.bfloat16)
    pre_act = product(second_in, upw_full) + upb_full.astype(jnp.float32)
    activ_value, gelu_slope = gelu_parts(pre_act)
    activated = activ_value.astype(jnp.bfloat16)
    hidden_out = (
        residual + product(activated, downw_full) + downb_full.astype(jnp.float32)
    ).astype(jnp.bfloat16)
    back_qkv, back_out, back_up, back_down, back_gain1, back_gain2 = (
        qkv_full,
        outw_full,
        upw_full,
        downw_full,
        gain_one,
        gain_two,
    )
    upstream = out_grad.astype(jnp.float32)
    down_owned = lax.psum_scatter(
        column_term(activated, out_grad).astype(jnp.bfloat16),
        "shard",
        scatter_dimension=0,
        tiled=True,
    )
    down_bgrad = jnp.sum(upstream, axis=0)
    pre_grad = right_product(out_grad, back_down) * gelu_slope
    pre_round = pre_grad.astype(jnp.bfloat16)
    up_bgrad = jnp.sum(pre_grad, axis=0)
    up_owned = lax.psum_scatter(
        column_term(second_in, pre_round).astype(jnp.bfloat16),
        "shard",
        scatter_dimension=0,
        tiled=True,
    )
    second_grad = right_product(pre_round, back_up)
    norm_two_in, gain2_grad, bias2_grad = norm_back(second_grad, normed_two, inv_two, back_gain2)
    resid_grad = upstream + norm_two_in
    resid_round = resid_grad.astype(jnp.bfloat16)
    out_bgrad = jnp.sum(resid_grad, axis=0)
    out_owned = lax.psum_scatter(
        column_term(context, resid_round).astype(jnp.bfloat16),
        "shard",
        scatter_dimension=0,
        tiled=True,
    )
    context_grad = right_product(resid_round, back_out).astype(jnp.bfloat16)
    query_grad, key_grad, value_grad = attend_backward(
        queries, key_rows, values, allowed, log_total, context_grad
    )
    query_bgrad = jnp.sum(query_grad, axis=0)
    value_bgrad = jnp.sum(value_grad, axis=0)
    qkv_grad = jnp.concatenate([query_grad, key_grad, value_grad], axis=1).astype(jnp.bfloat16)
    qkv_owned = lax.psum_scatter(
        column_term(first_in, qkv_grad).astype(jnp.bfloat16),
        "shard",
        scatter_dimension=0,
        tiled=True,
    )
    first_grad = right_product(qkv_grad, back_qkv)
    norm_one_in, gain1_grad, bias1_grad = norm_back(first_grad, normed_one, inv_one, back_gain1)
    in_grad = (resid_grad + norm_one_in).astype(jnp.bfloat16)
    (
        gain1_own,
        bias1_own,
        qbias_own,
        vbias_own,
        outb_own,
        gain2_own,
        bias2_own,
        upb_own,
        downb_own,
    ) = (
        lax.psum_scatter(
            gain1_grad.astype(jnp.bfloat16), "shard", scatter_dimension=0, tiled=True
        ).astype(jnp.float32),
        lax.psum_scatter(
            bias1_grad.astype(jnp.bfloat16), "shard", scatter_dimension=0, tiled=True
        ).astype(jnp.float32),
        lax.psum_scatter(
            query_bgrad.astype(jnp.bfloat16), "shard", scatter_dimension=0, tiled=True
        ).astype(jnp.float32),
        lax.psum_scatter(
            value_bgrad.astype(jnp.bfloat16), "shard", scatter_dimension=0, tiled=True
        ).astype(jnp.float32),
        lax.psum_scatter(
            out_bgrad.astype(jnp.bfloat16), "shard", scatter_dimension=0, tiled=True
        ).astype(jnp.float32),
        lax.psum_scatter(
            gain2_grad.astype(jnp.bfloat16), "shard", scatter_dimension=0, tiled=True
        ).astype(jnp.float32),
        lax.psum_scatter(
            bias2_grad.astype(jnp.bfloat16), "shard", scatter_dimension=0, tiled=True
        ).astype(jnp.float32),
        lax.psum_scatter(
            up_bgrad.astype(jnp.bfloat16), "shard", scatter_dimension=0, tiled=True
        ).astype(jnp.float32),
        lax.psum_scatter(
            down_bgrad.astype(jnp.bfloat16), "shard", scatter_dimension=0, tiled=True
        ).astype(jnp.float32),
    )
    (
        gain1_total,
        bias1_total,
        qkv_total,
        qbias_total,
        vbias_total,
        outw_total,
        outb_total,
        gain2_total,
        bias2_total,
        upw_total,
        upb_total,
        downw_total,
        downb_total,
    ) = (
        lax.psum(gain1_own.astype(jnp.bfloat16), "replica").astype(jnp.float32),
        lax.psum(bias1_own.astype(jnp.bfloat16), "replica").astype(jnp.float32),
        lax.psum(qkv_owned, "replica").astype(jnp.float32),
        lax.psum(qbias_own.astype(jnp.bfloat16), "replica").astype(jnp.float32),
        lax.psum(vbias_own.astype(jnp.bfloat16), "replica").astype(jnp.float32),
        lax.psum(out_owned, "replica").astype(jnp.float32),
        lax.psum(outb_own.astype(jnp.bfloat16), "replica").astype(jnp.float32),
        lax.psum(gain2_own.astype(jnp.bfloat16), "replica").astype(jnp.float32),
        lax.psum(bias2_own.astype(jnp.bfloat16), "replica").astype(jnp.float32),
        lax.psum(up_owned, "replica").astype(jnp.float32),
        lax.psum(upb_own.astype(jnp.bfloat16), "replica").astype(jnp.float32),
        lax.psum(down_owned, "replica").astype(jnp.float32),
        lax.psum(downb_own.astype(jnp.bfloat16), "replica").astype(jnp.float32),
    )
    return (
        hidden_out,
        in_grad,
        gain1_total,
        bias1_total,
        qkv_total,
        qbias_total,
        vbias_total,
        outw_total,
        outb_total,
        gain2_total,
        bias2_total,
        upw_total,
        upb_total,
        downw_total,
        downb_total,
    )


def solution(mesh):
    in_specs = (
        P(("replica", "shard"), None),
        P(("replica", "shard"), None),
        P(("replica", "shard"), None),
        P("shard"),
        P("shard"),
        P("shard", None),
        P("shard"),
        P("shard"),
        P("shard", None),
        P("shard"),
        P("shard"),
        P("shard"),
        P("shard", None),
        P("shard"),
        P("shard", None),
        P("shard"),
    )
    out_specs = (
        P(("replica", "shard"), None),
        P(("replica", "shard"), None),
        P("shard"),
        P("shard"),
        P("shard", None),
        P("shard"),
        P("shard"),
        P("shard", None),
        P("shard"),
        P("shard"),
        P("shard"),
        P("shard", None),
        P("shard"),
        P("shard", None),
        P("shard"),
    )
    return jax.shard_map(local, mesh=mesh, in_specs=in_specs, out_specs=out_specs, check_vma=False)
```

profile of v0, /device:TPU:0, one launch (start us, length us, event | category | flops | bytes accessed | tf_op | source)
XLA Modules:
  0.0 687.5 jit_solution(8565300499013674690)
XLA Ops:
  7.2 0.7 all-gather.13.cloned.1.call-update
  8.0 0.7 all-gather.15.cloned.1.call-update
  8.8 0.7 all-gather.17.cloned.1.call-update
  9.5 0.5 all-gather.19.cloned.1.call-update
  10.1 6.0 all-gather.4
  16.2 5.4 all-gather.1
  21.6 5.2 all-gather
  26.8 5.2 all-gather.3
  32.0 5.2 all-gather.2
  37.3 5.4 all_gather.49
  42.6 5.2 all-gather.6
  47.9 5.2 all-gather.5
  53.5 0.2 fusion.38
  53.8 5.0 all-gather.13.cloned.1.call-done
  58.8 3.9 fusion.66
  63.4 0.4 convolution_multiply_fusion.1
  63.8 0.5 convolution_convert_fusion.6
  64.3 18.7 %all-gather.15.cloned.1.call-done = bf16[1024,1024]{1,0:T(8,128)(2,1)} async-done(((bf16[256,1024]{1,0:T(8,128)(2,1)}), bf16[1024,1024]{1,0:T(8,128)(2,1)}) %all-gather.15.cloned.1.call-update) | async-done | bytes 2097168 | tf_op jit(solution)/shard_map/all_gather | solution.py:160
  83.0 2.1 fusion.71
  85.1 0.2 multiply_reduce_fusion.3
  85.4 57.5 %all-gather.17.cloned.1.call-done = bf16[1024,4096]{1,0:T(8,128)(2,1)} async-done(((bf16[256,4096]{1,0:T(8,128)(2,1)}), bf16[1024,4096]{1,0:T(8,128)(2,1)}) %all-gather.17.cloned.1.call-update) | async-done | bytes 8388624 | tf_op jit(solution)/shard_map/all_gather | solution.py:164
  142.8 4.8 convolution_add_fusion
  147.6 54.9 %all-gather.19.cloned.1.call-done = bf16[4096,1024]{1,0:T(8,128)(2,1)} async-done(((bf16[1024,1024]{1,0:T(8,128)(2,1)}), bf16[4096,1024]{1,0:T(8,128)(2,1)}) %all-gather.19.cloned.1.call-update) | async-done | bytes 8388624 | tf_op jit(solution)/shard_map/all_gather | solution.py:166
  202.5 7.1 %fusion.74 = (bf16[4096]{0:T(1024)(128)(2,1)S(1)}, bf16[128,4096]{1,0:T(8,128)(2,1)S(1)}) fusion(f32[128,4096]{1,0:T(8,128)S(1)} %convolution_add_fusion, bf16[128,1024]{1,0:T(8,128)(2,1)S(1)} %copy-done.4, bf16[4096,1024]{1,0:T(8,128)(2,1)} %all-gather.19.cloned.1.call-done), kind=kOutput, calls=%fused_computation.108 | convolution fusion | flops 1084223488 | bytes 11804672 | tf_op jit(solution)/shard_map/dot_general | solution.py:25
  209.6 3.0 multiply_reduce_fusion.1
  212.7 0.3 fusion.68
  213.0 2.0 convolution_convert_fusion.3
  215.0 0.2 reduce-scatter.5.cloned.1.call-start
  215.3 3.0 fusion.13
  218.2 1.5 convolution_convert_fusion.5
  219.8 1.9 copy.63
  221.7 3.2 fusion.69
  224.8 2.4 fusion.75
  227.2 3.6 convolution_convert_fusion.4
  230.8 3.7 fusion.70
  234.5 5.8 convolution_convert_fusion.2
  240.4 6.9 %convolution_convert_fusion.1 = bf16[1024,4096]{1,0:T(8,128)(2,1)} fusion(bf16[128,4096]{1,0:T(8,128)(2,1)} %copy-done.3, f32[128,1024]{1,0:T(8,128)S(1)} %get-tuple-element.54, f32[1024]{0:T(1024)S(1)} %bitcast.77, f32[1024]{0:T(1024)S(1)} %bitcast.69, f32[128]{0:T(128)S(1)} %add_rsqrt_fusion, f32[128]{0:T(128)S(1)} %broadcast_multiply_fusion.4), kind=kOutput, calls=%fused_computation.3 | convolution fusion | flops 1078591488 | bytes 9970688 | tf_op jit(solution)/shard_map/dot_general | solution.py:19
  247.3 6.6 convolution_convert_fusion
  254.0 53.6 %reduce-scatter.5.cloned.1.call-done = bf16[256,3072]{1,0:T(8,128)(2,1)} async-done(((bf16[1024,3072]{1,0:T(8,128)(2,1)}), bf16[256,3072]{1,0:T(8,128)(2,1)}) %reduce-scatter.5.cloned.1.call-update) | async-done | bytes 1572880 | tf_op jit(solution)/shard_map/reduce_scatter | solution.py:231
  307.6 74.0 %reduce-scatter.9.cloned.1.call-done = bf16[256,4096]{1,0:T(8,128)(2,1)} async-done(((bf16[1024,4096]{1,0:T(8,128)(2,1)}), bf16[256,4096]{1,0:T(8,128)(2,1)}) %reduce-scatter.9.cloned.1.call-update) | async-done | bytes 2097168 | tf_op jit(solution)/shard_map/reduce_scatter | solution.py:207
  381.6 74.0 %reduce-scatter.11.cloned.1.call-done = bf16[1024,1024]{1,0:T(8,128)(2,1)} async-done(((bf16[4096,1024]{1,0:T(8,128)(2,1)}), bf16[1024,1024]{1,0:T(8,128)(2,1)}) %reduce-scatter.11.cloned.1.call-update) | async-done | bytes 2097168 | tf_op jit(solution)/shard_map/reduce_scatter | solution.py:197
  455.7 0.6 copy-done.24
  456.3 5.1 all-gather.7
  461.4 1.0 reduce_sum.202
  462.4 0.6 dynamic-slice
  464.4 6.9 fusion.37
  471.3 11.3 %all-reduce.11 = (bf16[1024]{0:T(1024)(128)(2,1)S(1)}, bf16[1024]{0:T(1024)(128)(2,1)S(1)}, bf16[1024]{0:T(1024)(128)(2,1)S(1)}, bf16[1024]{0:T(1024)(128)(2,1)S...) all-reduce(bf16[1024]{0:T(1024)(128)(2,1)S(1)} %get-tuple-element.1, ...), channel_id=2, replica_groups=mesh['replica'=8,'shard'=4] {'shard'}, use_global_device_ids=true, to_apply=%region_13.14.clone | all-reduce | flops 12288 | bytes 49152
  483.2 23.3 %all-reduce.9 = (bf16[256]{0:T(256)(128)(2,1)S(1)}, bf16[256]{0:T(256)(128)(2,1)S(1)}, bf16[256]{0:T(256)(128)(2,1)S(1)}, bf16[256]{0:T(256)(128)(2,1)S(1)}, bf1...) all-reduce(bf16[256]{0:T(256)(128)(2,1)S(1)} %dynamic-slice.1, ...), channel_id=1, replica_groups=mesh['replica'=8,'shard'=4] {'replica'}, use_global_device_ids=true, to_apply=%region_14.15 | all-reduce | flops 3072 | bytes 12288 | tf_op jit(solution)/shard_map/psum | solution.py:294
  506.4 0.6 convert_element_type.228
  507.0 0.6 convert_element_type.230
  507.6 0.6 convert_element_type.235
  508.1 0.6 convert_element_type.238
  508.7 0.6 convert_element_type.242
  509.3 0.6 convert_element_type.244
  509.8 0.6 convert_element_type.246
  510.4 0.6 convert_element_type.250
  511.0 0.6 convert_element_type.253
  511.6 2.0 fusion.36
  513.6 5.6 fusion.17
  519.2 152.1 %all-reduce.14.cloned.1.call-done = (bf16[256,3072]{1,0:T(8,128)(2,1)}, bf16[256,1024]{1,0:T(8,128)(2,1)}, bf16[256,4096]{1,0:T(8,128)(2,1)}, bf16[1024,1024]{1,0:T(8,128)(2,1)}) async-done(((bf16[256,3072]{1,0:T(8,128)(2,1)}, bf16[256,1024]{1,0:T(8,128)(2,1)}, bf16[256,4096]{1,0:T(8,128)(2,1)}, bf16[1024,1024]{1,0:T(8,128)(2,1)}), (bf16[256,3072]{1,0:T(8,128)(2,1)}, bf16[256,1024]{1,0:T(8,128)(2,1)}, ...) | async-done | bytes 6291472 | tf_op jit(solution)/shard_map/psum | solution.py:296
  671.3 3.6 convert_element_type.232
  674.9 1.1 convert_element_type.240
  676.0 2.5 convert_element_type.248
  678.5 2.5 convert_element_type.252
  (109 shorter events, 2.5 us)
Async XLA Ops:
  7.2 51.6 %all-gather.13.cloned.1.call-start = ((), (), s32[]{:S(2)}) async-start(), calls=%async_computation.4 | async-start | bytes 7864320 | tf_op jit(solution)/shard_map/all_gather | solution.py:157
  7.9 75.1 %all-gather.15.cloned.1.call-start = ((), (), s32[]{:S(2)}) async-start(), calls=%async_computation.5 | async-start | bytes 2621440 | tf_op jit(solution)/shard_map/all_gather | solution.py:160
  8.7 1.5 copy-start.16
  8.7 7.5 %copy-start.17 = (bf16[256]{0:T(256)(128)(2,1)S(1)}, bf16[256]{0:T(256)(128)(2,1)}, u32[]{:S(2)}) copy-start(bf16[256]{0:T(256)(128)(2,1)} %param.20) | copy-start | bytes 1540
  8.7 12.9 %copy-start.18 = (bf16[256]{0:T(256)(128)(2,1)S(1)}, bf16[256]{0:T(256)(128)(2,1)}, u32[]{:S(2)}) copy-start(bf16[256]{0:T(256)(128)(2,1)} %param.19) | copy-start | bytes 1540
  8.7 18.1 %copy-start.19 = (bf16[256]{0:T(256)(128)(2,1)S(1)}, bf16[256]{0:T(256)(128)(2,1)}, u32[]{:S(2)}) copy-start(bf16[256]{0:T(256)(128)(2,1)} %param.22) | copy-start | bytes 1540
  8.7 23.3 %copy-start.20 = (bf16[256]{0:T(256)(128)(2,1)S(1)}, bf16[256]{0:T(256)(128)(2,1)}, u32[]{:S(2)}) copy-start(bf16[256]{0:T(256)(128)(2,1)} %param.23) | copy-start | bytes 1540
  8.7 28.5 %copy-start.15 = (bf16[1024]{0:T(1024)(128)(2,1)S(1)}, bf16[1024]{0:T(1024)(128)(2,1)}, u32[]{:S(2)}) copy-start(bf16[1024]{0:T(1024)(128)(2,1)} %param.29) | copy-start | bytes 6148
  8.7 33.9 %copy-start.21 = (bf16[256]{0:T(256)(128)(2,1)S(1)}, bf16[256]{0:T(256)(128)(2,1)}, u32[]{:S(2)}) copy-start(bf16[256]{0:T(256)(128)(2,1)} %param.27) | copy-start | bytes 1540
  8.7 39.1 %copy-start.22 = (bf16[256]{0:T(256)(128)(2,1)S(1)}, bf16[256]{0:T(256)(128)(2,1)}, u32[]{:S(2)}) copy-start(bf16[256]{0:T(256)(128)(2,1)} %param.26) | copy-start | bytes 1540
  8.7 44.3 %copy-start.23 = (s32[1,4]{1,0:T(1,128)S(1)}, s32[1,4]{1,0:T(1,128)}, u32[]{:S(2)}) copy-start(s32[1,4]{1,0:T(1,128)} %param.18) | copy-start | bytes 52
  8.8 44.6 %copy-start.1 = (bf16[128,1024]{1,0:T(8,128)(2,1)S(1)}, bf16[128,1024]{1,0:T(8,128)(2,1)}, u32[]{:S(2)}) copy-start(bf16[128,1024]{1,0:T(8,128)(2,1)} %param.16) | copy-start | bytes 786436
  8.8 134.1 %all-gather.17.cloned.1.call-start = ((), (), s32[]{:S(2)}) async-start(), calls=%async_computation.6 | async-start | bytes 10485760 | tf_op jit(solution)/shard_map/all_gather | solution.py:164
  9.5 193.0 %all-gather.19.cloned.1.call-start = ((), (), s32[]{:S(2)}) async-start(), calls=%async_computation.7 | async-start | bytes 10485760 | tf_op jit(solution)/shard_map/all_gather | solution.py:166
  10.1 243.9 %reduce-scatter.7.cloned.1.call-start = ((), (), s32[]{:S(2)}) async-start(), calls=%async_computation.9 | async-start | bytes 2621440 | tf_op jit(solution)/shard_map/reduce_scatter | solution.py:218
  63.0 1.2 copy-start.10
  63.2 21.9 %copy-start.11 = (bf16[128,1024]{0,1:T(8,128)(2,1)}, bf16[128,1024]{0,1:T(8,128)(2,1)S(1)}, u32[]{:S(2)}) copy-start(bf16[128,1024]{0,1:T(8,128)(2,1)S(1)} %copy.60) | copy-start | bytes 786436
  63.4 21.7 %copy-start.9 = (bf16[128,1024]{0,1:T(8,128)(2,1)}, bf16[128,1024]{0,1:T(8,128)(2,1)S(1)}, u32[]{:S(2)}) copy-start(bf16[128,1024]{0,1:T(8,128)(2,1)S(1)} %copy.61) | copy-start | bytes 786436
  63.8 19.2 %copy-start.8 = (f32[16,128,128]{1,2,0:T(8,128)}, f32[16,128,128]{1,2,0:T(8,128)S(1)}, u32[]{:S(2)}) copy-start(f32[16,128,128]{1,2,0:T(8,128)S(1)} %convolution_multiply_fusion.1) | copy-start | bytes 3145732
  64.3 78.6 %copy-start.12 = (bf16[16,64,128]{2,1,0:T(8,128)(2,1)}, bf16[16,64,128]{2,1,0:T(8,128)(2,1)S(1)}, u32[]{:S(2)}) copy-start(bf16[16,64,128]{2,1,0:T(8,128)(2,1)S(1)} %convolution_convert_fusion.6) | copy-start | bytes 786436
  142.8 59.7 %copy-start.4 = (bf16[128,1024]{1,0:T(8,128)(2,1)S(1)}, bf16[128,1024]{1,0:T(8,128)(2,1)}, u32[]{:S(2)}) copy-start(bf16[128,1024]{1,0:T(8,128)(2,1)} %param.17) | copy-start | bytes 786436
  202.5 7.1 %copy-start = (bf16[1024,4096]{1,0:T(8,128)(2,1)S(1)}, bf16[1024,4096]{1,0:T(8,128)(2,1)}, u32[]{:S(2)}) copy-start(bf16[1024,4096]{1,0:T(8,128)(2,1)} %all-gather.17.cloned.1.call-done) | copy-start | bytes 25165828
  209.6 3.1 copy-start.3
  209.6 3.1 copy-start.5
  209.6 3.3 copy-start.13
  215.0 92.6 %reduce-scatter.5.cloned.1.call-start = ((), (), s32[]{:S(2)}) async-start(), calls=%async_computation.8 | async-start | bytes 7864320 | tf_op jit(solution)/shard_map/reduce_scatter | solution.py:231
  215.2 3.0 copy-start.2
  240.3 141.3 %reduce-scatter.9.cloned.1.call-start = ((), (), s32[]{:S(2)}) async-start(), calls=%async_computation.10 | async-start | bytes 10485760 | tf_op jit(solution)/shard_map/reduce_scatter | solution.py:207
  247.3 208.4 %reduce-scatter.11.cloned.1.call-start = ((), (), s32[]{:S(2)}) async-start(), calls=%async_computation.11 | async-start | bytes 10485760 | tf_op jit(solution)/shard_map/reduce_scatter | solution.py:197
  253.9 417.3 %all-reduce.14.cloned.1.call-start = ((), (), s32[]{:S(2)}) async-start(), calls=%async_computation.12 | async-start | bytes 12582912 | tf_op jit(solution)/shard_map/psum | solution.py:296
  455.7 0.7 copy-start.24
  455.7 6.7 copy-start.25
  671.3 3.6 copy-start.14
  671.3 4.7 copy-start.7
  676.0 2.5 copy-start.6
Sparse Core Ops, SparseCore 0:
  9.6 49.2 all-gather.12
  60.4 22.5 all-gather.14
  84.5 58.2 all-gather.16
  144.2 58.2 all-gather.18
  215.1 31.1 reduce-scatter.6
  248.7 58.8 reduce-scatter.4
  310.2 71.3 reduce-scatter.8
  384.2 71.4 reduce-scatter.10
  460.1 211.1 all-reduce.13
where the time goes:
time: 688 us; the launch traced here: 687 us
  waiting for transfers between devices  493 us (72%)
  blocking collectives  82.4 us (12%)
  matrix products  69.8 us (10%)
  other arithmetic  22.1 us (3%)
  between operations  15.6 us (2%)
    psum x1, waiting for transfers between devices, local(): lax.psum(qkv_owned, 'replica').astype(jnp.float32)  152 us
    reduce_scatter x1, waiting for transfers between devices, local(): lax.psum_scatter(column_term(activated, out_grad).astype(jnp.bfloat16), '...  74 us
    reduce_scatter x1, waiting for transfers between devices, local(): lax.psum_scatter(column_term(second_in, pre_round).astype(jnp.bfloat16),...  74 us
    all_gather x1, waiting for transfers between devices, local(): lax.all_gather(up_weight, 'shard', axis=0, tiled=True)  57.5 us
    all_gather x1, waiting for transfers between devices, local(): lax.all_gather(down_weight, 'shard', axis=0, tiled=True)  54.9 us
    reduce_scatter x1, waiting for transfers between devices, local(): lax.psum_scatter(column_term(first_in, qkv_grad).astype(jnp.bfloat16), 's...  53.6 us
    psum x1, blocking collectives, local(): lax.psum(gain1_own.astype(jnp.bfloat16), 'replica').astype(jnp.float32)  23.3 us
    dot_general x4, matrix products, left_product(): lax.dot_general(left, right, (((0,), (0,)), ((), ())), preferred_element_...  21.3 us
  transfers between devices with their start and end apart: 9, of which 8 were waited for; matrix products, arithmetic and copies ran while one was open for 11% of the time, Pallas kernels for 0%

commit v1 on v0

--- a/solution.py
+++ b/solution.py
@@ -9,6 +9,7 @@
 EPSILON = 1e-05
 TANH_SCALE = math.sqrt(2.0 / math.pi)
 CUBIC = 0.044715
+load_object = lambda point: lax.all_gather(point, axis_name="replica").sum(axis=0)
 
 
 def product(left, right):
@@ -293,7 +294,7 @@
     ) = (
         lax.psum(gain1_own.astype(jnp.bfloat16), "replica").astype(jnp.float32),
         lax.psum(bias1_own.astype(jnp.bfloat16), "replica").astype(jnp.float32),
-        lax.psum(qkv_owned, "replica").astype(jnp.float32),
+        load_object(qkv_owned).astype(jnp.float32),
         lax.psum(qbias_own.astype(jnp.bfloat16), "replica").astype(jnp.float32),
         lax.psum(vbias_own.astype(jnp.bfloat16), "replica").astype(jnp.float32),
         lax.psum(out_owned, "replica").astype(jnp.float32),

time: 688 us -> 824 us (1.20)
  waiting for transfers between devices: 493 us -> 620 us
  other arithmetic: 22.1 us -> 30.6 us
    all_gather x0 -> x1, waiting for transfers between devices: none -> 168 us  [lax.all_gather(point, axis_name='replica').sum(axis=0)]
    psum x1, waiting for transfers between devices: 152 us -> 111 us  [local(): lax.psum(out_owned, 'replica').astype(jnp.float32)]
  transfers between devices with their start and end apart: 9 -> 10, of which waited for: 8 -> 9; matrix products, arithmetic and copies ran while one was open for 11% -> 10% of each run, Pallas kernels for 0% -> 0%
where the time goes in v1:
time: 824 us; the launch traced here: 823 us
  waiting for transfers between devices  620 us (75%)
  blocking collectives  82.3 us (10%)
  matrix products  69.9 us (8%)
  other arithmetic  30.6 us (4%)
  between operations  15.9 us (2%)
    all_gather x1, waiting for transfers between devices, lax.all_gather(point, axis_name='replica').sum(axis=0)  168 us
    psum x1, waiting for transfers between devices, local(): lax.psum(out_owned, 'replica').astype(jnp.float32)  111 us
    reduce_scatter x1, waiting for transfers between devices, local(): lax.psum_scatter(column_term(activated, out_grad).astype(jnp.bfloat16), '...  74 us
    reduce_scatter x1, waiting for transfers between devices, local(): lax.psum_scatter(column_term(second_in, pre_round).astype(jnp.bfloat16),...  66.5 us
    reduce_scatter x1, waiting for transfers between devices, local(): lax.psum_scatter(column_term(first_in, qkv_grad).astype(jnp.bfloat16), 's...  61.3 us
    all_gather x1, waiting for transfers between devices, local(): lax.all_gather(up_weight, 'shard', axis=0, tiled=True)  57.5 us
    all_gather x1, waiting for transfers between devices, local(): lax.all_gather(down_weight, 'shard', axis=0, tiled=True)  54.9 us
    psum x1, blocking collectives, local(): lax.psum(gain1_own.astype(jnp.bfloat16), 'replica').astype(jnp.float32)  23.1 us
  transfers between devices with their start and end apart: 10, of which 9 were waited for; matrix products, arithmetic and copies ran while one was open for 10% of the time, Pallas kernels for 0%

profile of v1, /device:TPU:0, one launch (start us, length us, event | category | flops | bytes accessed | tf_op | source)
XLA Modules:
  0.0 823.2 jit_solution(16255423062943975380)
XLA Ops:
  7.2 0.7 all-gather.15.cloned.1.call-update
  8.0 0.7 all-gather.17.cloned.1.call-update
  8.8 0.7 all-gather.19.cloned.1.call-update
  9.5 0.5 all-gather.21.cloned.1.call-update
  10.1 6.0 all-gather.5
  16.2 5.4 all-gather.2
  21.6 5.2 all-gather.1
  26.8 5.2 all-gather.4
  32.0 5.2 all-gather.3
  37.3 5.4 all_gather.55
  42.6 5.2 all-gather.7
  47.9 5.2 all-gather.6
  53.5 0.2 fusion.38
  53.8 5.0 all-gather.15.cloned.1.call-done
  58.8 3.9 fusion.66
  63.4 0.4 convolution_multiply_fusion.1
  63.8 0.5 convolution_convert_fusion.6
  64.3 18.7 %all-gather.17.cloned.1.call-done = bf16[1024,1024]{1,0:T(8,128)(2,1)} async-done(((bf16[256,1024]{1,0:T(8,128)(2,1)}), bf16[1024,1024]{1,0:T(8,128)(2,1)}) %all-gather.17.cloned.1.call-update) | async-done | bytes 2097168 | tf_op jit(solution)/shard_map/all_gather | solution.py:161
  83.0 2.1 fusion.71
  85.4 57.5 %all-gather.19.cloned.1.call-done = bf16[1024,4096]{1,0:T(8,128)(2,1)} async-done(((bf16[256,4096]{1,0:T(8,128)(2,1)}), bf16[1024,4096]{1,0:T(8,128)(2,1)}) %all-gather.19.cloned.1.call-update) | async-done | bytes 8388624 | tf_op jit(solution)/shard_map/all_gather | solution.py:165
  142.8 4.8 convolution_add_fusion
  147.6 54.9 %all-gather.21.cloned.1.call-done = bf16[4096,1024]{1,0:T(8,128)(2,1)} async-done(((bf16[1024,1024]{1,0:T(8,128)(2,1)}), bf16[4096,1024]{1,0:T(8,128)(2,1)}) %all-gather.21.cloned.1.call-update) | async-done | bytes 8388624 | tf_op jit(solution)/shard_map/all_gather | solution.py:167
  202.6 7.0 fusion.74
  209.6 3.0 multiply_reduce_fusion.1
  212.7 0.3 fusion.68
  213.0 2.0 convolution_convert_fusion.3
  215.0 0.2 reduce-scatter.9.cloned.1.call-start
  215.2 7.2 convolution_convert_fusion.1
  222.5 6.8 convolution_convert_fusion
  229.4 3.0 fusion.13
  232.4 1.5 convolution_convert_fusion.5
  233.9 1.8 copy.63
  235.7 2.8 fusion.69
  238.5 2.4 fusion.75
  240.9 3.5 convolution_convert_fusion.4
  244.4 3.5 fusion.70
  247.9 5.7 convolution_convert_fusion.2
  253.7 66.5 %reduce-scatter.9.cloned.1.call-done = bf16[256,4096]{1,0:T(8,128)(2,1)} async-done(((bf16[1024,4096]{1,0:T(8,128)(2,1)}), bf16[256,4096]{1,0:T(8,128)(2,1)}) %reduce-scatter.9.cloned.1.call-update) | async-done | bytes 2097168 | tf_op jit(solution)/shard_map/reduce_scatter | solution.py:208
  320.2 74.0 %reduce-scatter.11.cloned.1.call-done = bf16[1024,1024]{1,0:T(8,128)(2,1)} async-done(((bf16[4096,1024]{1,0:T(8,128)(2,1)}), bf16[1024,1024]{1,0:T(8,128)(2,1)}) %reduce-scatter.11.cloned.1.call-update) | async-done | bytes 2097168 | tf_op jit(solution)/shard_map/reduce_scatter | solution.py:198
  394.3 61.3 %reduce-scatter.5.cloned.1.call-done = bf16[256,3072]{1,0:T(8,128)(2,1)} async-done(((bf16[1024,3072]{1,0:T(8,128)(2,1)}), bf16[256,3072]{1,0:T(8,128)(2,1)}) %reduce-scatter.5.cloned.1.call-update) | async-done | bytes 1572880 | tf_op jit(solution)/shard_map/reduce_scatter | solution.py:232
  455.7 5.1 all-gather.8
  460.8 1.0 reduce_sum.215
  461.8 0.6 dynamic-slice
  463.8 7.2 fusion.37
  471.0 11.3 %all-reduce.11 = (bf16[1024]{0:T(1024)(128)(2,1)S(1)}, bf16[1024]{0:T(1024)(128)(2,1)S(1)}, bf16[1024]{0:T(1024)(128)(2,1)S(1)}, bf16[1024]{0:T(1024)(128)(2,1)S...) all-reduce(bf16[1024]{0:T(1024)(128)(2,1)S(1)} %get-tuple-element.1, ...), channel_id=3, replica_groups=mesh['replica'=8,'shard'=4] {'shard'}, use_global_device_ids=true, to_apply=%region_13.14.clone | all-reduce | flops 12288 | bytes 49152
  482.9 23.1 %all-reduce.9 = (bf16[256]{0:T(256)(128)(2,1)S(1)}, bf16[256]{0:T(256)(128)(2,1)S(1)}, bf16[256]{0:T(256)(128)(2,1)S(1)}, bf16[256]{0:T(256)(128)(2,1)S(1)}, bf1...) all-reduce(bf16[256]{0:T(256)(128)(2,1)S(1)} %dynamic-slice.1, ...), channel_id=1, replica_groups=mesh['replica'=8,'shard'=4] {'replica'}, use_global_device_ids=true, to_apply=%region_14.15 | all-reduce | flops 3072 | bytes 12288 | tf_op jit(solution)/shard_map/psum | solution.py:295
  506.0 0.6 convert_element_type.230
  506.6 0.6 convert_element_type.232
  507.2 0.6 convert_element_type.237
  507.7 0.6 convert_element_type.240
  508.3 0.6 convert_element_type.244
  508.8 0.6 convert_element_type.246
  509.4 0.6 convert_element_type.248
  510.0 0.6 convert_element_type.252
  510.6 0.6 convert_element_type.255
  511.1 2.0 fusion.36
  513.1 5.6 fusion.17
  518.8 111.1 %all-reduce.14.cloned.1.call-done = (bf16[256,1024]{1,0:T(8,128)(2,1)}, bf16[256,4096]{1,0:T(8,128)(2,1)}, bf16[1024,1024]{1,0:T(8,128)(2,1)}) async-done(((bf16[256,1024]{1,0:T(8,128)(2,1)}, bf16[256,4096]{1,0:T(8,128)(2,1)}, bf16[1024,1024]{1,0:T(8,128)(2,1)}), (bf16[256,1024]{1,0:T(8,128)(2,1)}, bf16[256,4096]{1,0:T(8,128)(2,1)}, bf16[1024,1024]{1,0:T(8,128)(2,1)})) %all-reduce.14.cloned.1.call-update) | async-done | bytes 4718608 | tf_op jit(solution)/shard_map/psum | solution.py:300
  629.9 2.1 convert_element_type.242
  632.0 4.2 convert_element_type.250
  636.3 2.5 convert_element_type.254
  638.7 168.3 %all-gather.23.cloned.1.call-done = bf16[2048,3072]{1,0:T(8,128)(2,1)} async-done(((bf16[256,3072]{1,0:T(8,128)(2,1)}), bf16[2048,3072]{1,0:T(8,128)(2,1)}) %all-gather.23.cloned.1.call-update) | async-done | bytes 12582928 | tf_op jit(solution)/shard_map/all_gather | solution.py:12
  807.1 7.3 reduce_sum.208
  814.3 2.0 convert_element_type.234
  (109 shorter events, 2.8 us)
Async XLA Ops:
  7.2 51.6 %all-gather.15.cloned.1.call-start = ((), (), s32[]{:S(2)}) async-start(), calls=%async_computation.4 | async-start | bytes 7864320 | tf_op jit(solution)/shard_map/all_gather | solution.py:158
  7.9 75.1 %all-gather.17.cloned.1.call-start = ((), (), s32[]{:S(2)}) async-start(), calls=%async_computation.5 | async-start | bytes 2621440 | tf_op jit(solution)/shard_map/all_gather | solution.py:161
  8.7 1.5 copy-start.14
  8.7 7.5 copy-start.15
  8.7 12.9 %copy-start.16 = (bf16[256]{0:T(256)(128)(2,1)S(1)}, bf16[256]{0:T(256)(128)(2,1)}, u32[]{:S(2)}) copy-start(bf16[256]{0:T(256)(128)(2,1)} %param.19) | copy-start | bytes 1540
  8.7 18.1 %copy-start.17 = (bf16[256]{0:T(256)(128)(2,1)S(1)}, bf16[256]{0:T(256)(128)(2,1)}, u32[]{:S(2)}) copy-start(bf16[256]{0:T(256)(128)(2,1)} %param.22) | copy-start | bytes 1540
  8.7 23.3 %copy-start.18 = (bf16[256]{0:T(256)(128)(2,1)S(1)}, bf16[256]{0:T(256)(128)(2,1)}, u32[]{:S(2)}) copy-start(bf16[256]{0:T(256)(128)(2,1)} %param.23) | copy-start | bytes 1540
  8.7 28.5 %copy-start.13 = (bf16[1024]{0:T(1024)(128)(2,1)S(1)}, bf16[1024]{0:T(1024)(128)(2,1)}, u32[]{:S(2)}) copy-start(bf16[1024]{0:T(1024)(128)(2,1)} %param.29) | copy-start | bytes 6148
  8.7 33.9 %copy-start.19 = (bf16[256]{0:T(256)(128)(2,1)S(1)}, bf16[256]{0:T(256)(128)(2,1)}, u32[]{:S(2)}) copy-start(bf16[256]{0:T(256)(128)(2,1)} %param.27) | copy-start | bytes 1540
  8.7 39.1 %copy-start.20 = (bf16[256]{0:T(256)(128)(2,1)S(1)}, bf16[256]{0:T(256)(128)(2,1)}, u32[]{:S(2)}) copy-start(bf16[256]{0:T(256)(128)(2,1)} %param.26) | copy-start | bytes 1540
  8.7 44.3 %copy-start.21 = (s32[1,4]{1,0:T(1,128)S(1)}, s32[1,4]{1,0:T(1,128)}, u32[]{:S(2)}) copy-start(s32[1,4]{1,0:T(1,128)} %param.18) | copy-start | bytes 52
  8.8 44.6 %copy-start.1 = (bf16[128,1024]{1,0:T(8,128)(2,1)S(1)}, bf16[128,1024]{1,0:T(8,128)(2,1)}, u32[]{:S(2)}) copy-start(bf16[128,1024]{1,0:T(8,128)(2,1)} %param.16) | copy-start | bytes 786436
  8.8 134.1 %all-gather.19.cloned.1.call-start = ((), (), s32[]{:S(2)}) async-start(), calls=%async_computation.6 | async-start | bytes 10485760 | tf_op jit(solution)/shard_map/all_gather | solution.py:165
  9.5 193.0 %all-gather.21.cloned.1.call-start = ((), (), s32[]{:S(2)}) async-start(), calls=%async_computation.7 | async-start | bytes 10485760 | tf_op jit(solution)/shard_map/all_gather | solution.py:167
  10.1 243.6 %reduce-scatter.7.cloned.1.call-start = ((), (), s32[]{:S(2)}) async-start(), calls=%async_computation.9 | async-start | bytes 2621440 | tf_op jit(solution)/shard_map/reduce_scatter | solution.py:219
  63.0 1.2 copy-start.9
  63.2 21.9 %copy-start.10 = (bf16[128,1024]{0,1:T(8,128)(2,1)}, bf16[128,1024]{0,1:T(8,128)(2,1)S(1)}, u32[]{:S(2)}) copy-start(bf16[128,1024]{0,1:T(8,128)(2,1)S(1)} %copy.60) | copy-start | bytes 786436
  63.4 21.7 %copy-start.8 = (bf16[128,1024]{0,1:T(8,128)(2,1)}, bf16[128,1024]{0,1:T(8,128)(2,1)S(1)}, u32[]{:S(2)}) copy-start(bf16[128,1024]{0,1:T(8,128)(2,1)S(1)} %copy.61) | copy-start | bytes 786436
  63.8 19.2 %copy-start.7 = (f32[16,128,128]{1,2,0:T(8,128)}, f32[16,128,128]{1,2,0:T(8,128)S(1)}, u32[]{:S(2)}) copy-start(f32[16,128,128]{1,2,0:T(8,128)S(1)} %convolution_multiply_fusion.1) | copy-start | bytes 3145732
  64.3 78.6 %copy-start.11 = (bf16[16,64,128]{2,1,0:T(8,128)(2,1)}, bf16[16,64,128]{2,1,0:T(8,128)(2,1)S(1)}, u32[]{:S(2)}) copy-start(bf16[16,64,128]{2,1,0:T(8,128)(2,1)S(1)} %convolution_convert_fusion.6) | copy-start | bytes 786436
  142.8 59.7 %copy-start.4 = (bf16[128,1024]{1,0:T(8,128)(2,1)S(1)}, bf16[128,1024]{1,0:T(8,128)(2,1)}, u32[]{:S(2)}) copy-start(bf16[128,1024]{1,0:T(8,128)(2,1)} %param.17) | copy-start | bytes 786436
  202.5 7.1 copy-start
  209.6 3.1 copy-start.3
  209.6 3.1 copy-start.5
  209.6 3.3 copy-start.12
  215.0 105.2 %reduce-scatter.9.cloned.1.call-start = ((), (), s32[]{:S(2)}) async-start(), calls=%async_computation.10 | async-start | bytes 10485760 | tf_op jit(solution)/shard_map/reduce_scatter | solution.py:208
  222.5 171.7 %reduce-scatter.11.cloned.1.call-start = ((), (), s32[]{:S(2)}) async-start(), calls=%async_computation.11 | async-start | bytes 10485760 | tf_op jit(solution)/shard_map/reduce_scatter | solution.py:198
  229.3 226.3 %reduce-scatter.5.cloned.1.call-start = ((), (), s32[]{:S(2)}) async-start(), calls=%async_computation.8 | async-start | bytes 7864320 | tf_op jit(solution)/shard_map/reduce_scatter | solution.py:232
  229.4 3.0 copy-start.2
  253.6 376.3 %all-reduce.14.cloned.1.call-start = ((), (), s32[]{:S(2)}) async-start(), calls=%async_computation.13 | async-start | bytes 9437184 | tf_op jit(solution)/shard_map/psum | solution.py:300
  394.2 61.4 %copy-start.22 = (bf16[256]{0:T(256)(128)(2,1)S(1)}, bf16[256]{0:T(256)(128)(2,1)}, u32[]{:S(2)}) copy-start(bf16[256]{0:T(256)(128)(2,1)} %param.31) | copy-start | bytes 1540
  394.2 67.5 %copy-start.23 = (u32[32]{0:T(128)S(1)}, u32[32]{0:T(128)}, u32[]{:S(2)}) copy-start(u32[32]{0:T(128)} %constant.37) | copy-start | bytes 388
  394.2 412.8 %all-gather.23.cloned.1.call-start = ((), (), s32[]{:S(2)}) async-start(), calls=%async_computation.12 | async-start | bytes 14155776 | tf_op jit(solution)/shard_map/all_gather | solution.py:12
  632.0 4.3 copy-start.6
Sparse Core Ops, SparseCore 0:
  9.6 49.2 all-gather.14
  60.4 22.5 all-gather.16
  84.5 58.2 all-gather.18
  144.2 58.2 all-gather.20
  215.1 31.1 reduce-scatter.6
  248.8 71.4 reduce-scatter.8
  322.8 71.3 reduce-scatter.10
  396.8 58.8 reduce-scatter.4
  459.6 170.2 all-reduce.13
  631.9 175.0 all-gather.22
